TPU v7x, 32 devices: a whole 2x2x4 slice. The times are simulated.
32 devices in a mesh: groups: 2 (over x), row: 16 (over z, y, core).
Axes of the slice: x: 2, y: 2, z: 4, core: 2. Of those that a mesh axis runs over, the one named last changes fastest.
Arguments:
- exterior_map: bfloat16 [15360, 7680], P(('groups', 'row')), parts along dimension 0, may hold values from -6 to 6
- couple_maps: bfloat16 [4, 7680, 1024], P('groups', 'row'), parts along dimension 0, may hold values from -0.1875 to 0.1875
- face_from_exterior: bfloat16 [15360, 1024], P(('groups', 'row')), parts along dimension 0, may hold values from -12 to 12
- face_maps: float32 [4096, 1024], P(('groups', 'row')), parts along dimension 0, may hold values from -1 to 2
- start_inverse: float32 [2048, 1024], P('groups'), parts along dimension 0, may hold values from -1 to 1
Outputs:
- merged_columns: bfloat16 [2, 15360, 7680], P(None, ('groups', 'row')), parts along dimension 1
There are 2 independent parts, one for each index of `groups`. A program takes and returns all parts, laid end to end along the dimension named above; each array names one. Nothing has to cross between parts.
All inputs are finite; a program needn't handle non-finite values.
Results may differ from a plain program's by a relative error of at most 0.0095.
Values may be sent and summed in bfloat16 or wider, within the bound.
No kernel may reach another device: no remote copies, remote signals or barrier semaphores. Data moves between devices by JAX's collectives and lax.ppermute only.
A program may use at most 128 MiB of HBM per device.

v0:
```python
import jax
import jax.numpy as jnp
from jax import lax
from jax.sharding import PartitionSpec as P

NEWTON = 2


def shifted(block, axis, distance):
    devices = range(lax.axis_size(axis))
    route = [((i - distance) % len(devices), i) for i in devices]
    return lax.ppermute(block, axis, route)


def per_device(exterior_map, couple_maps, face_from_exterior, face_maps, start_inverse):
    high = lax.Precision.HIGHEST
    devices = lax.axis_size("row")
    position = lax.axis_index("row")
    halfway = devices // 2
    face_rows = face_maps.shape[0] // 2
    width = start_inverse.shape[0]
    sibling_side = position // halfway
    own_block = lax.dynamic_slice_in_dim(face_maps, sibling_side * face_rows, face_rows, 0)
    received = shifted(face_maps.astype(jnp.bfloat16), "row", halfway).astype(face_maps.dtype)
    coupling = own_block + lax.dynamic_slice_in_dim(
        received, sibling_side * face_rows, face_rows, 0
    )
    own_start = 2 * face_rows * (position % halfway) + face_rows * sibling_side

    def reorder(gathered):
        return (
            gathered.reshape(2, halfway, face_rows, width)
            .transpose(1, 0, 2, 3)
            .reshape(width, width)
        )

    iterate = start_inverse
    product = iterate
    for newton_step in range(NEWTON):
        product_rows = jnp.dot(
            coupling, iterate, precision=high, preferred_element_type=jnp.float32
        )
        product = reorder(lax.all_gather(product_rows, "row", axis=0, tiled=True))
        if newton_step + 1 < NEWTON:
            my_rows = lax.dynamic_slice_in_dim(iterate, own_start, face_rows, 0)
            next_rows = 2.0 * my_rows - jnp.dot(
                my_rows, product, precision=high, preferred_element_type=jnp.float32
            )
            iterate = reorder(
                lax.all_gather(next_rows.astype(jnp.bfloat16), "row", axis=0, tiled=True).astype(
                    next_rows.dtype
                )
            )
    panel_rows = face_from_exterior.astype(jnp.float32)
    contract = (((1,), (1,)), ((), ()))
    direct = lax.dot_general(
        panel_rows, iterate, contract, precision=high, preferred_element_type=jnp.float32
    )
    through = lax.dot_general(
        panel_rows, product, contract, precision=high, preferred_element_type=jnp.float32
    )
    image_rows = 2.0 * direct - lax.dot_general(
        through, iterate, contract, precision=high, preferred_element_type=jnp.float32
    )
    image_rows = image_rows.astype(jnp.bfloat16)
    own_cols = exterior_map.astype(jnp.float32)
    update = jnp.einsum(
        "bis,es->bie",
        couple_maps,
        lax.all_gather(image_rows, "row", axis=0, tiled=True),
        preferred_element_type=jnp.float32,
    )
    return jnp.stack([own_cols - update[0], -update[1]]).astype(jnp.bfloat16)


def solution(mesh):
    return jax.shard_map(
        per_device,
        mesh=mesh,
        in_specs=(
            P(("groups", "row"), None),
            P("groups", "row", None),
            P(("groups", "row"), None),
            P(("groups", "row"), None),
            P("groups", None),
        ),
        out_specs=P(None, ("groups", "row"), None),
        check_vma=False,
    )
```

profile of v0, /device:TPU:0, one launch (start us, length us, event | category | flops | bytes accessed | tf_op | source)
XLA Modules:
  0.0 370.7 jit_solution(8878733400885816180)
XLA Ops:
  6.5 0.0 copy-start
  6.5 0.0 all-gather.5.cloned.1.call-start
  6.5 1.2 convert_element_type.19
  7.8 4.1 %collective-permute-start = (bf16[128,1024]{1,0:T(8,128)(2,1)S(1)}, bf16[128,1024]{1,0:T(8,128)(2,1)S(1)}, u32[]{:S(2)}, u32[]{:S(2)}) collective-permute-start(bf16[128,1024]{1,0:T(8,128)(2,1)S(1)} %convert_element_type.19), channel_id=1, source_target_pairs={{8,0},{9,1},{10,2},{11,3},{12,4},{13,5},{14,6},{15,7},{0,8},{1,9},... | collective-permute-start | bytes 786440 | tf_op jit(solution)/shard_map/ppermute | solution.py:12
  11.9 11.9 %collective-permute-done = bf16[128,1024]{1,0:T(8,128)(2,1)S(1)} collective-permute-done((bf16[128,1024]{1,0:T(8,128)(2,1)S(1)}, bf16[128,1024]{1,0:T(8,128)(2,1)S(1)}, u32[]{:S(2)}, u32[]{:S(2)}) %collective-permute-start) | collective-permute-done | bytes 262176 | tf_op jit(solution)/shard_map/ppermute | solution.py:12
  23.8 5.6 %fusion.9 = f32[64,1024]{1,0:T(8,128)} fusion(f32[1024,1024]{1,0:T(8,128)} %param.9, f32[128,1024]{1,0:T(8,128)} %param.8, s32[]{:T(128)S(6)} %select_n.21, bf16[128,1024]{1,0:T(8,128)(2,1)S(1)} %collective-permute-done), kind=kOutput, calls=%fused_computation.16 | convolution fusion | flops 805437440 | bytes 4849668 | tf_op jit(solution)/shard_map/dot_general | solution.py:40
  29.4 0.0 all-gather.5.cloned.1.call-update
  29.5 0.0 all-gather.7.cloned.1.call-start
  29.5 51.6 %all-gather.5.cloned.1.call-done = f32[1024,1024]{1,0:T(8,128)} async-done(((f32[64,1024]{1,0:T(8,128)}), f32[1024,1024]{1,0:T(8,128)}) %all-gather.5.cloned.1.call-update) | async-done | bytes 4194320 | tf_op jit(solution)/shard_map/all_gather | solution.py:43
  81.2 2.5 copy.6
  83.7 0.0 copy-start.5
  83.7 4.4 %fusion.6 = bf16[64,1024]{1,0:T(8,128)(2,1)} fusion(f32[1024,1024]{1,0:T(8,128)S(1)} %bitcast.42, f32[1024,1024]{1,0:T(8,128)} %param.9, s32[]{:T(128)S(6)} %select_n.20), kind=kOutput, calls=%fused_computation.12 | convolution fusion | flops 805502976 | bytes 4850688 | tf_op jit(solution)/shard_map/dot_general | solution.py:46
  88.1 0.0 all-gather.7.cloned.1.call-update
  88.1 0.0 all-gather.9.cloned.1.call-start
  88.2 40.1 %all-gather.7.cloned.1.call-done = bf16[1024,1024]{1,0:T(8,128)(2,1)} async-done(((bf16[64,1024]{1,0:T(8,128)(2,1)}), bf16[1024,1024]{1,0:T(8,128)(2,1)}) %all-gather.7.cloned.1.call-update) | async-done | bytes 2097168 | tf_op jit(solution)/shard_map/all_gather | solution.py:50
  128.3 1.8 copy.7
  130.0 0.0 copy-start.3
  130.0 1.3 copy-done.3
  131.3 0.0 copy-done.5
  131.3 1.9 fusion.8
  133.3 0.0 all-gather.9.cloned.1.call-update
  133.3 0.2 all-gather.11.cloned.1.call-start
  133.5 49.0 %all-gather.9.cloned.1.call-done = f32[1024,1024]{1,0:T(8,128)} async-done(((f32[64,1024]{1,0:T(8,128)}), f32[1024,1024]{1,0:T(8,128)}) %all-gather.9.cloned.1.call-update) | async-done | bytes 4194320 | tf_op jit(solution)/shard_map/all_gather | solution.py:43
  182.6 0.0 copy-start.6
  182.6 2.6 copy.8
  185.2 0.0 copy-start.4
  185.2 0.0 copy-done.6
  185.2 3.4 fusion.15
  188.6 0.0 copy-done.4
  188.6 6.7 %fusion.16 = f32[480,1024]{1,0:T(8,128)S(1)} fusion(f32[1024,480]{1,0:T(8,128)S(1)} %fusion.15, bf16[1024,1024]{1,0:T(8,128)(2,1)S(1)} %bitcast.44), kind=kOutput, calls=%fused_computation.23 | convolution fusion | flops 6039797760 | bytes 6029312 | tf_op jit(solution)/shard_map/dot_general | solution.py:62
  195.4 2.2 fusion.5
  197.6 0.0 all-gather.11.cloned.1.call-update
  197.6 118.5 %all-gather.11.cloned.1.call-done = bf16[7680,1024]{1,0:T(8,128)(2,1)} async-done(((bf16[480,1024]{1,0:T(8,128)(2,1)}), bf16[7680,1024]{1,0:T(8,128)(2,1)}) %all-gather.11.cloned.1.call-update) | async-done | bytes 15728656 | tf_op jit(solution)/shard_map/all_gather | solution.py:70
  316.1 0.0 copy-done
  316.1 22.8 %convolution_bitcast_fusion = f32[2,480,7680]{2,1,0:T(8,128)} fusion(bf16[2,480,1024]{2,1,0:T(8,128)(2,1)S(1)} %copy-done, bf16[7680,1024]{1,0:T(8,128)(2,1)} %all-gather.11.cloned.1.call-done), kind=kOutput, calls=%fused_computation | convolution fusion | flops 15099494400 | bytes 47185920 | tf_op jit(solution)/shard_map/bis,es->bie/dot_general | solution.py:67
  338.9 9.6 %fusion.1 = bf16[1,480,7680]{2,1,0:T(8,128)(2,1)} fusion(f32[2,480,7680]{2,1,0:T(8,128)} %convolution_bitcast_fusion), kind=kLoop, calls=%fused_computation.3 | loop fusion | flops 7372800 | bytes 22118400 | tf_op jit(solution)/shard_map/convert.1
  348.5 0.0 copy-start.2
  348.5 8.1 %fusion.4 = bf16[1,480,7680]{2,1,0:T(8,128)(2,1)S(1)} fusion(f32[2,480,7680]{2,1,0:T(8,128)} %convolution_bitcast_fusion, bf16[480,7680]{1,0:T(8,128)(2,1)} %param.5), kind=kLoop, calls=%fused_computation.8 | loop fusion | flops 11059200 | bytes 29491200 | tf_op jit(solution)/shard_map/stack | solution.py:73
  356.6 1.4 copy-done.2
  358.0 0.0 copy-start.1
  358.0 6.2 %pad_maximum_fusion = bf16[2,480,7680]{2,1,0:T(8,128)(2,1)} fusion(bf16[1,480,7680]{2,1,0:T(8,128)(2,1)S(1)} %copy-done.2, bf16[1,480,7680]{2,1,0:T(8,128)(2,1)S(1)} %fusion.4), kind=kLoop, calls=%fused_computation.7 | loop fusion | flops 7372800 | bytes 29491200 | tf_op jit(solution)/shard_map/stack | solution.py:73
  364.2 0.0 copy-done.1
Async XLA Ops:
  6.5 309.6 %copy-start = (bf16[2,480,1024]{2,1,0:T(8,128)(2,1)S(1)}, bf16[2,480,1024]{2,1,0:T(8,128)(2,1)}, u32[]{:S(2)}) copy-start(bf16[2,480,1024]{2,1,0:T(8,128)(2,1)} %param.6) | copy-start | bytes 5898244
  6.5 74.6 %all-gather.5.cloned.1.call-start = ((), (), s32[]{:S(2)}) async-start(), calls=%async_computation | async-start | bytes 4456448 | tf_op jit(solution)/shard_map/all_gather | solution.py:43
  7.8 16.1 %collective-permute-start = (bf16[128,1024]{1,0:T(8,128)(2,1)S(1)}, bf16[128,1024]{1,0:T(8,128)(2,1)S(1)}, u32[]{:S(2)}, u32[]{:S(2)}) collective-permute-start(bf16[128,1024]{1,0:T(8,128)(2,1)S(1)} %convert_element_type.19), channel_id=1, source_target_pairs={{8,0},{9,1},{10,2},{11,3},{12,4},{13,5},{14,6},{15,7},{0,8},{1,9},... | collective-permute-start | bytes 786440 | tf_op jit(solution)/shard_map/ppermute | solution.py:12
  29.5 98.8 %all-gather.7.cloned.1.call-start = ((), (), s32[]{:S(2)}) async-start(), calls=%async_computation.1 | async-start | bytes 2228224 | tf_op jit(solution)/shard_map/all_gather | solution.py:50
  83.7 47.7 %copy-start.5 = (f32[128,1024]{1,0:T(8,128)S(1)}, f32[128,1024]{1,0:T(8,128)}, u32[]{:S(2)}) copy-start(f32[128,1024]{1,0:T(8,128)} %param.8) | copy-start | bytes 1572868
  88.1 94.5 %all-gather.9.cloned.1.call-start = ((), (), s32[]{:S(2)}) async-start(), calls=%async_computation.2 | async-start | bytes 4456448 | tf_op jit(solution)/shard_map/all_gather | solution.py:43
  130.0 1.3 copy-start.3
  133.3 182.8 %all-gather.11.cloned.1.call-start = ((), (), s32[]{:S(2)}) async-start(), calls=%async_computation.3 | async-start | bytes 16711680 | tf_op jit(solution)/shard_map/all_gather | solution.py:70
  182.6 2.6 copy-start.6
  185.2 3.5 copy-start.4
  348.5 9.5 %copy-start.2 = (bf16[1,480,7680]{2,1,0:T(8,128)(2,1)S(1)}, bf16[1,480,7680]{2,1,0:T(8,128)(2,1)}, u32[]{:S(2)}) copy-start(bf16[1,480,7680]{2,1,0:T(8,128)(2,1)} %fusion.1) | copy-start | bytes 22118404
  358.0 6.2 %copy-start.1 = (bf16[2,480,1024]{2,1,0:T(8,128)(2,1)S(1)}, bf16[2,480,1024]{2,1,0:T(8,128)(2,1)}, u32[]{:S(2)}) copy-start(bf16[2,480,1024]{2,1,0:T(8,128)(2,1)} %param.6) | copy-start | bytes 5898244
Sparse Core Ops, SparseCore 0:
  29.6 51.5 all-gather.4
  88.2 39.9 all-gather.6
  133.4 49.0 all-gather.8
  197.7 118.3 all-gather.10
where the time goes:
time: 371 us
  waiting for transfers between devices  271 us (73%)
  matrix products  47.1 us (13%)
  other arithmetic  25.1 us (7%)
  between operations  13.2 us (4%)
  local copies, waits for them, and re-layouts  9.56 us (3%)
  starting transfers between devices  4.44 us (1%)
    all_gather x1, waiting for transfers between devices, per_device(): lax.all_gather(image_rows, 'row', axis=0, tiled=True)  119 us
    all_gather x2, waiting for transfers between devices, per_device(): product = reorder(lax.all_gather(product_rows, 'row', axis=0, tiled=True))  101 us
    all_gather x1, waiting for transfers between devices, per_device(): lax.all_gather(next_rows.astype(jnp.bfloat16), 'row', axis=0, tiled=True)  40.1 us
    dot_general x1, matrix products, per_device(): jnp.einsum('bis,es->bie', couple_maps, lax.all_gather(image_rows, 'row',...  22.8 us
    another operation x2, other arithmetic, per_device(): return jnp.stack([own_cols - update[0], -update[1]]).astype(jnp.bfloat16)  14.3 us
    ppermute x1, waiting for transfers between devices, shifted(): return lax.ppermute(block, axis, route)  11.9 us
    another operation x1, other arithmetic  9.64 us
    dot_general x2, matrix products, per_device(): jnp.dot(coupling, iterate, precision=high, preferred_element_type=jnp.flo...  7.57 us
  transfers between devices with their start and end apart: 5, of which 5 were waited for; matrix products, arithmetic and copies ran while one was open for 0% of the time, Pallas kernels for 0%

commit v1 on v0

v1 whole, which is shorter than its diff:
```python
import functools
import math

import jax
import jax.numpy as jnp
from jax import lax
from jax.experimental import pallas as pl
from jax.experimental.pallas import tpu as pltpu
from jax.sharding import PartitionSpec as P

NT = (((1,), (1,)), ((), ()))
BF16 = jnp.bfloat16
F32 = jnp.float32


def ring_order(chips):
    return list(range(0, chips, 2)) + list(range(chips - 1, 0, -2))


def ring_chip(place, chips):
    place = lax.rem(place + 2 * chips, chips)
    return jnp.where(place < chips // 2, 2 * place, 2 * (chips - 1 - place) + 1)


def ring_place(chip, chips):
    return jnp.where(chip % 2 == 0, chip // 2, chips - 1 - (chip - 1) // 2)


def chain_kernel(rows, tab, base, *refs):
    pieces = refs[:-5]
    out, full, wide, narrow, sem = refs[-5:]
    loads = [
        pltpu.make_async_copy(
            piece.at[pl.ds(k * rows, rows), :],
            full.at[pl.ds(pl.multiple_of(tab[2 * i + k], rows), rows), :],
            sem.at[2 * i + k],
        )
        for i, piece in enumerate(pieces)
        for k in range(2)
    ]
    for load in loads:
        load.start()
    narrow[0] = base[...].astype(BF16)
    for load in loads:
        load.wait()
    size = full.shape[1]
    tile = math.gcd(size, 256)
    cols = lambda j: pl.ds(pl.multiple_of(j * tile, tile), tile)

    @pl.loop(0, size // tile)
    def _(j):
        first = base[:, cols(j)] + jnp.dot(
            narrow[0], full[:, cols(j)], preferred_element_type=F32
        )
        wide[:, cols(j)] = first
        narrow[1, :, cols(j)] = first.astype(BF16)

    @pl.loop(0, size // tile)
    def _(j):
        narrow[0, :, cols(j)] = jnp.dot(
            narrow[1], full[:, cols(j)], preferred_element_type=F32
        ).astype(BF16)

    @pl.loop(0, size // tile)
    def _(j):
        out[:, cols(j)] = (
            wide[:, cols(j)]
            + jnp.dot(narrow[0], full[:, cols(j)], preferred_element_type=F32)
        ).astype(BF16)


def chain(tab, base, pieces, rows):
    m, size = base.shape
    vmem = pl.BlockSpec(memory_space=pltpu.VMEM)
    return pl.pallas_call(
        functools.partial(chain_kernel, rows),
        out_shape=jax.ShapeDtypeStruct((m, size), BF16),
        in_specs=[pl.BlockSpec(memory_space=pltpu.SMEM), vmem]
        + [pl.BlockSpec(memory_space=pl.ANY)] * len(pieces),
        out_specs=vmem,
        scratch_shapes=[
            pltpu.VMEM((size, size), BF16),
            pltpu.VMEM((m, size), F32),
            pltpu.VMEM((2, m, size), BF16),
            pltpu.SemaphoreType.DMA((2 * len(pieces),)),
        ],
        compiler_params=pltpu.CompilerParams(vmem_limit_bytes=36 * 2**20),
        cost_estimate=pl.CostEstimate(
            flops=6 * m * size * size, bytes_accessed=8 * m * size, transcendentals=0
        ),
        name="chain",
    )(tab, base, *pieces)


def stage_kernel(count, windows, olds, tab, *refs):
    refs = list(refs)
    take = lambda n: [refs.pop(0) for _ in range(n)]
    pieces = take(count)
    mixed, own = take(2) if windows else (None, None)
    take(olds)
    (full,) = take(1)
    (out,) = take(1) if windows else (None,)
    if count:
        bounce, in_sem, out_sem = take(3)
        rows = pieces[0].shape[0]
        ins = [
            pltpu.make_async_copy(pieces[i], bounce.at[i], in_sem.at[i])
            for i in range(count)
        ]
        outs = [
            pltpu.make_async_copy(
                bounce.at[i],
                full.at[pl.ds(pl.multiple_of(tab[i], 16), rows), :],
                out_sem.at[i],
            )
            for i in range(count)
        ]
        for copy in ins:
            copy.start()
        for i in range(count):
            ins[i].wait()
            outs[i].start()
        for copy in outs:
            copy.wait()
    if not windows:
        return
    panel, held, done, load_sem, store_sem = take(5)
    width = panel.shape[1]
    tile = math.gcd(width, 256)

    def cols(i):
        return pl.ds(pl.multiple_of(tab[count + i], 128), width)

    def loads(i, slot):
        return (
            pltpu.make_async_copy(
                full.at[cols(i), :], panel.at[slot], load_sem.at[0, slot]
            ),
            pltpu.make_async_copy(
                own.at[:, cols(i)], held.at[slot], load_sem.at[1, slot]
            ),
        )

    def store(i, slot):
        return pltpu.make_async_copy(
            done.at[slot], out.at[:, :, cols(i)], store_sem.at[slot]
        )

    for copy in loads(0, 0):
        copy.start()

    @pl.loop(0, windows)
    def _(i):
        slot = lax.rem(i, 2)

        @pl.when(i + 1 < windows)
        def _():
            for copy in loads(i + 1, 1 - slot):
                copy.start()

        for copy in loads(i, slot):
            copy.wait()

        for j in range(width // tile):
            span = pl.ds(j * tile, tile)
            part = panel[slot, span, :]
            upper = lax.dot_general(mixed[0], part, NT, preferred_element_type=F32)
            done[slot, 0, :, span] = (
                held[slot, :, span].astype(F32) - upper
            ).astype(BF16)
            lower = lax.dot_general(mixed[1], part, NT, preferred_element_type=F32)
            done[slot, 1, :, span] = (-lower).astype(BF16)

        @pl.when(i > 0)
        def _():
            store(i - 1, 1 - slot).wait()

        store(i, slot).start()

    store(windows - 1, (windows - 1) % 2).wait()


def stage(tab, pieces, full, mixed=None, own=None, out=None, windows=0, width=0, total=0):
    count = len(pieces)
    hbm = pl.BlockSpec(memory_space=pl.ANY)
    args = [tab, *pieces]
    in_specs = [pl.BlockSpec(memory_space=pltpu.SMEM)] + [hbm] * count
    shapes = [jax.ShapeDtypeStruct((total, pieces[0].shape[1]), BF16)] if full is None else [
        jax.ShapeDtypeStruct(full.shape, BF16)
    ]
    size = shapes[0].shape[1]
    scratch = []
    if count:
        scratch += [
            pltpu.VMEM((count, *pieces[0].shape), BF16),
            pltpu.SemaphoreType.DMA((count,)),
            pltpu.SemaphoreType.DMA((count,)),
        ]
    if windows:
        maps, mine = mixed.shape[:2]
        args += [mixed, own]
        in_specs += [pl.BlockSpec(memory_space=pltpu.VMEM), hbm]
        shapes.append(jax.ShapeDtypeStruct((maps, mine, own.shape[1]), BF16))
        scratch += [
            pltpu.VMEM((2, width, size), BF16),
            pltpu.VMEM((2, mine, width), BF16),
            pltpu.VMEM((2, maps, mine, width), BF16),
            pltpu.SemaphoreType.DMA((2, 2)),
            pltpu.SemaphoreType.DMA((2,)),
        ]
    olds = [(old, k) for k, old in enumerate((full, out)) if old is not None]
    aliases = {len(args) + i: k for i, (_, k) in enumerate(olds)}
    args += [old for old, _ in olds]
    in_specs += [hbm] * len(olds)
    flops = windows * 4 * (mixed.shape[1] if windows else 0) * size * width
    moved = 4 * sum(p.size for p in pieces) + windows * width * (size + 3 * size) * 2
    return pl.pallas_call(
        functools.partial(stage_kernel, count, windows, len(olds)),
        out_shape=shapes,
        in_specs=in_specs,
        out_specs=[hbm] * len(shapes),
        scratch_shapes=scratch,
        input_output_aliases=aliases,
        compiler_params=pltpu.CompilerParams(vmem_limit_bytes=24 * 2**20),
        cost_estimate=pl.CostEstimate(
            flops=flops, bytes_accessed=moved, transcendentals=0
        ),
        name="stage",
    )(*args)


def per_device(exterior_map, couple_maps, face_from_exterior, face_maps, start_inverse):
    high = lax.Precision.HIGHEST
    devices = lax.axis_size("row")
    chips = devices // 2
    half = chips // 2
    me = lax.axis_index("row")
    chip, core = me // 2, me % 2
    place = ring_place(chip, chips)
    size = start_inverse.shape[0]
    order = ring_order(chips)

    ring_pairs = []
    for i in range(chips):
        ring_pairs.append((2 * order[i], 2 * order[(i + 1) % chips]))
        ring_pairs.append((2 * order[i] + 1, 2 * order[i - 1] + 1))
    hop = lambda block: lax.ppermute(block, "row", ring_pairs)
    swap = lambda block: lax.ppermute(block, "row", [(i, i ^ 1) for i in range(devices)])
    far = lambda block: lax.ppermute(
        block, "row", [(i, (i + chips) % devices) for i in range(devices)]
    )

    face_rows = face_maps.shape[0] // 2
    side = me // chips
    keep = lax.dynamic_slice_in_dim(face_maps, side * face_rows, face_rows, 0)
    give = lax.dynamic_slice_in_dim(face_maps, (1 - side) * face_rows, face_rows, 0)
    coupling = keep + far(give.astype(BF16)).astype(F32)

    def residual_start(device):
        return 2 * face_rows * (device % chips) + face_rows * (device // chips)

    eye = (
        lax.broadcasted_iota(jnp.int32, (face_rows, size), 1)
        == lax.broadcasted_iota(jnp.int32, (face_rows, size), 0) + residual_start(me)
    ).astype(F32)
    residual = (
        eye - jnp.dot(coupling, start_inverse, precision=high, preferred_element_type=F32)
    ).astype(BF16)

    away = jnp.where(core == 0, -1, 1)

    def shard_at(steps, own_core):
        return 2 * ring_chip(place + steps, chips) + own_core

    pair = jnp.concatenate([residual, swap(residual)], axis=0)
    residual_pieces = [pair]
    residual_shards = [me, me ^ 1]
    block = pair
    for step in range(1, half + 1):
        block = hop(block)
        residual_pieces.append(block)
        residual_shards += [
            shard_at(away * step, core),
            shard_at(away * step, 1 - core),
        ]
        if step < half:
            residual_pieces.append(swap(block))
            residual_shards += [
                shard_at(-away * step, 1 - core),
                shard_at(-away * step, core),
            ]

    rows = face_from_exterior.shape[0]
    first, second = face_from_exterior, swap(face_from_exterior)
    groups = [([first, second], [me, me ^ 1], [chip])]
    for step in range(1, half + 1):
        blocks, shards = [], []
        first = hop(first)
        blocks += [first, swap(first)]
        shards += [shard_at(away * step, core), shard_at(-away * step, 1 - core)]
        if step < half:
            second = hop(second)
            blocks += [second, swap(second)]
            shards += [shard_at(away * step, 1 - core), shard_at(-away * step, core)]
            both = [ring_chip(place + step, chips), ring_chip(place - step, chips)]
        else:
            both = [ring_chip(place + step, chips)]
        groups.append((blocks, shards, both))

    maps, mine = couple_maps.shape[:2]
    left = couple_maps.reshape(maps * mine, size)
    upper_part = lax.reduce_precision(start_inverse, 8, 7)
    lower_part = (start_inverse - upper_part).astype(BF16)
    base = jnp.dot(left, upper_part.astype(BF16), preferred_element_type=F32) + jnp.dot(
        left, lower_part, preferred_element_type=F32
    )
    starts = jnp.stack([residual_start(d) for d in residual_shards]).astype(jnp.int32)
    mixed = chain(starts, base, residual_pieces, face_rows).reshape(maps, mine, size)

    span = 2 * rows
    total = devices * rows
    width = -(-(span + 128 - math.gcd(span, 128)) // 128) * 128

    def table(shards, chips_done):
        starts = [shard * rows for shard in shards] + [
            jnp.minimum(c * span // 128 * 128, total - width) for c in chips_done
        ]
        return jnp.stack(starts).astype(jnp.int32)

    full = out = None
    early = []
    for step, (blocks, shards, done) in enumerate(groups):
        if step < half - 1:
            (full,) = stage(table(shards, []), blocks, full, total=total)
            early += done
        else:
            if step == half - 1:
                full, out = stage(
                    table([], early), [], full, mixed, exterior_map, out, len(early), width
                )
            full, out = stage(
                table(shards, done), blocks, full, mixed, exterior_map, out, len(done), width
            )
    return out


def solution(mesh):
    return jax.shard_map(
        per_device,
        mesh=mesh,
        in_specs=(
            P(("groups", "row"), None),
            P("groups", "row", None),
            P(("groups", "row"), None),
            P(("groups", "row"), None),
            P("groups", None),
        ),
        out_specs=P(None, ("groups", "row"), None),
        check_vma=False,
    )
```

time: 371 us -> 160 us (0.43)
  waiting for transfers between devices: 271 us -> 45.7 us
  Pallas kernels: 0 us -> 50.4 us
  matrix products: 47.1 us -> 11.3 us
  other arithmetic: 25.1 us -> 0.32 us
  starting transfers between devices: 4.44 us -> 26.6 us
  local copies, waits for them, and re-layouts: 9.56 us -> 24.5 us
  between operations: 13.2 us -> 0.5 us
    all_gather x4 -> x0, waiting for transfers between devices: 259 us -> none  [the longest x1 119 us: per_device(): lax.all_gather(image_rows, 'row', axis=0, tiled=True)]
    pallas_call x0 -> x7, Pallas kernels: none -> 50.4 us  [the longest x6 38.6 us: stage(): pl.pallas_call(functools.partial(stage_kernel, count, windows, len(olds))...]
    dot_general x7 -> x3, matrix products: 47.1 us -> 11.3 us  [the longest x1 4.93 us: per_device(): jnp.dot(coupling, start_inverse, precision=high, preferred_element_type=F32)]
    ppermute x1 -> x24, waiting for transfers between devices: 11.9 us -> 45.7 us  [the longest x11 35.6 us: per_device(): hop = lambda block: lax.ppermute(block, 'row', ring_pairs)]
    another operation x3 -> x4, other arithmetic: 23.9 us -> 0.3 us  [table(): return jnp.stack(starts).astype(jnp.int32)]
    ppermute x1 -> x24, starting transfers between devices: 4.13 us -> 26.6 us  [the longest x11 17.5 us: per_device(): hop = lambda block: lax.ppermute(block, 'row', ring_pairs)]
    unnamed x14 -> x60, local copies, waits for them, and re-layouts: 2.73 us -> 23.3 us
    reshape x3 -> x0, local copies, waits for them, and re-layouts: 6.84 us -> none  [reorder(): gathered.reshape(2, halfway, face_rows, width).transpose(1, 0, 2, 3)]
  transfers between devices with their start and end apart: 5 -> 24, of which waited for: 5 -> 7; matrix products, arithmetic and copies ran while one was open for 0% -> 8% of each run, Pallas kernels for 0% -> 28%
where the time goes in v1:
time: 160 us; the launch traced here: 159 us
  Pallas kernels  50.4 us (32%)
  waiting for transfers between devices  45.7 us (29%)
  starting transfers between devices  26.6 us (17%)
  local copies, waits for them, and re-layouts  24.5 us (15%)
  matrix products  11.3 us (7%)
    pallas_call x6, Pallas kernels, stage(): pl.pallas_call(functools.partial(stage_kernel, count, windows, len(olds))...  38.6 us
    ppermute x11, waiting for transfers between devices, per_device(): hop = lambda block: lax.ppermute(block, 'row', ring_pairs)  35.6 us
    unnamed x60, local copies, waits for them, and re-layouts  23.3 us
    ppermute x11, starting transfers between devices, per_device(): hop = lambda block: lax.ppermute(block, 'row', ring_pairs)  17.5 us
    pallas_call x1, Pallas kernels, chain(): pl.pallas_call(functools.partial(chain_kernel, rows), out_shape=jax.Shape...  11.8 us
    ppermute x1, waiting for transfers between devices, per_device(): lax.ppermute(block, 'row', [(i, (i + chips) % devices) for i in range(dev...  9.47 us
    ppermute x12, starting transfers between devices, per_device(): lax.ppermute(block, 'row', [(i, i ^ 1) for i in range(devices)])  6.41 us
    dot_general x1, matrix products, per_device(): jnp.dot(coupling, start_inverse, precision=high, preferred_element_type=F32)  4.93 us
  transfers between devices with their start and end apart: 24, of which 7 were waited for; matrix products, arithmetic and copies ran while one was open for 8% of the time, Pallas kernels for 28%

profile of v1, /device:TPU:0, one launch (start us, length us, event | category | flops | bytes accessed | tf_op | source)
XLA Modules:
  0.0 159.3 jit_solution(7843090467662143196)
XLA Ops:
  0.0 0.5 collective-permute-start.15
  0.5 2.6 %collective-permute-start = (bf16[480,1024]{1,0:T(8,128)(2,1)}, bf16[480,1024]{1,0:T(8,128)(2,1)}, u32[]{:S(2)}, u32[]{:S(2)}) collective-permute-start(bf16[480,1024]{1,0:T(8,128)(2,1)} %refs_0_.1), channel_id=1, source_target_pairs={{0,4},{1,3},{4,8},{5,1},{8,12},{9,5},{12,14},{13,9},{14,10},{15,13... | collective-permute-start | bytes 2949128 | tf_op jit(solution)/shard_map/ppermute | solution.py:247
  3.1 1.0 dynamic-slice_convert_fusion
  4.1 2.7 %collective-permute-start.5 = (bf16[64,1024]{1,0:T(8,128)(2,1)S(1)}, bf16[64,1024]{1,0:T(8,128)(2,1)S(1)}, u32[]{:S(2)}, u32[]{:S(2)}) collective-permute-start(bf16[64,1024]{1,0:T(8,128)(2,1)S(1)} %dynamic-slice_convert_fusion), channel_id=1, source_target_pairs={{0,8},{1,9},{2,10},{3,11},{4,12},{5,13},{6,14},{7,15},{8,0},{9,1},... | collective-permute-start | bytes 393224 | tf_op jit(solution)/shard_map/ppermute | solution.py:249
  6.7 0.0 collective-permute-done.15.refs_1_
  6.8 1.6 collective-permute-start.16
  8.3 9.5 %collective-permute-done.5 = bf16[64,1024]{1,0:T(8,128)(2,1)S(1)} collective-permute-done((bf16[64,1024]{1,0:T(8,128)(2,1)S(1)}, bf16[64,1024]{1,0:T(8,128)(2,1)S(1)}, u32[]{:S(2)}, u32[]{:S(2)}) %collective-permute-start.5) | collective-permute-done | bytes 131104 | tf_op jit(solution)/shard_map/ppermute | solution.py:249
  17.8 4.9 %fusion.4 = bf16[64,1024]{1,0:T(8,128)(2,1)S(1)} fusion(f32[1024,1024]{1,0:T(8,128)} %param.9, bf16[64,1024]{1,0:T(8,128)(2,1)S(1)} %collective-permute-done.5, f32[128,1024]{1,0:T(8,128)} %param.8, s32[]{:T(128)S(6)} %select_n.288, s32[64]{0:T(128)S(1)} %iota_add_fusion), kind=kOutput, calls=%fused_computation.7 | convolution fusion | flops 805699584 | bytes 4718852 | tf_op jit(solution)/shard_map/dot_general | solution.py:267
  22.7 4.1 %collective-permute-start.6 = (bf16[64,1024]{1,0:T(8,128)(2,1)S(1)}, bf16[64,1024]{1,0:T(8,128)(2,1)S(1)}, u32[]{:S(2)}, u32[]{:S(2)}) collective-permute-start(bf16[64,1024]{1,0:T(8,128)(2,1)S(1)} %fusion.4), channel_id=1, source_target_pairs={{0,1},{1,0},{2,3},{3,2},{4,5},{5,4},{6,7},{7,6},{8,9},{9,8},{10,11... | collective-permute-start | bytes 393224 | tf_op jit(solution)/shard_map/ppermute | solution.py:248
  26.9 0.0 collective-permute-done.refs_0_
  26.9 0.4 collective-permute-start.1
  27.2 0.6 collective-permute-done.6
  27.9 0.7 collective-permute-start.7
  28.6 0.7 copy-done.12
  29.3 14.9 %collective-permute-done.7.refs_1_ = bf16[128,1024]{1,0:T(8,128)(2,1)S(1)} collective-permute-done((bf16[128,1024]{1,0:T(8,128)(2,1)S(1)}, bf16[128,1024]{1,0:T(8,128)(2,1)S(1)}, u32[]{:S(2)}, u32[]{:S(2)}) %collective-permute-start.7) | collective-permute-done | bytes 262176 | tf_op jit(solution)/shard_map/ppermute | solution.py:247
  44.3 1.8 %collective-permute-start.9 = (bf16[128,1024]{1,0:T(8,128)(2,1)S(1)}, bf16[128,1024]{1,0:T(8,128)(2,1)S(1)}, u32[]{:S(2)}, u32[]{:S(2)}) collective-permute-start(bf16[128,1024]{1,0:T(8,128)(2,1)S(1)} %collective-permute-done.7.refs_1_), channel_id=1, source_target_pairs={{0,4},{1,3},{4,8},{5,1},{8,12},{9,5},{12,14},{13,9},{14,10},{15,13... | collective-permute-start | bytes 786440 | tf_op jit(solution)/shard_map/ppermute | solution.py:247
  46.1 2.5 %collective-permute-start.17 = (bf16[480,1024]{1,0:T(8,128)(2,1)}, bf16[480,1024]{1,0:T(8,128)(2,1)}, u32[]{:S(2)}, u32[]{:S(2)}) collective-permute-start(bf16[480,1024]{1,0:T(8,128)(2,1)} %collective-permute-done.16.refs_2_), channel_id=1, source_target_pairs={{0,4},{1,3},{4,8},{5,1},{8,12},{9,5},{12,14},{13,9},{14,10},{15,13... | collective-permute-start | bytes 2949128 | tf_op jit(solution)/shard_map/ppermute | solution.py:247
  48.5 0.0 collective-permute-start.8
  48.5 0.7 copy-done.14
  49.3 1.4 collective-permute-done.9.refs_3_
  50.6 1.8 %collective-permute-start.11 = (bf16[128,1024]{1,0:T(8,128)(2,1)S(1)}, bf16[128,1024]{1,0:T(8,128)(2,1)}, u32[]{:S(2)}, u32[]{:S(2)}) collective-permute-start(bf16[128,1024]{1,0:T(8,128)(2,1)S(1)} %collective-permute-done.9.refs_3_), channel_id=1, source_target_pairs={{0,4},{1,3},{4,8},{5,1},{8,12},{9,5},{12,14},{13,9},{14,10},{15,13... | collective-permute-start | bytes 786440 | tf_op jit(solution)/shard_map/ppermute | solution.py:247
  52.4 0.7 copy-done.18
  53.2 0.5 collective-permute-start.22
  53.7 10.4 %collective-permute-done.11.refs_5_ = bf16[128,1024]{1,0:T(8,128)(2,1)} collective-permute-done((bf16[128,1024]{1,0:T(8,128)(2,1)S(1)}, bf16[128,1024]{1,0:T(8,128)(2,1)}, u32[]{:S(2)}, u32[]{:S(2)}) %collective-permute-start.11) | collective-permute-done | bytes 262176 | tf_op jit(solution)/shard_map/ppermute | solution.py:247
  64.1 1.8 %collective-permute-start.2 = (bf16[480,1024]{1,0:T(8,128)(2,1)}, bf16[480,1024]{1,0:T(8,128)(2,1)}, u32[]{:S(2)}, u32[]{:S(2)}) collective-permute-start(bf16[480,1024]{1,0:T(8,128)(2,1)} %collective-permute-done.1.refs_0_), channel_id=1, source_target_pairs={{0,4},{1,3},{4,8},{5,1},{8,12},{9,5},{12,14},{13,9},{14,10},{15,13... | collective-permute-start | bytes 2949128 | tf_op jit(solution)/shard_map/ppermute | solution.py:247
  65.9 2.2 %fusion.1 = f32[1024,960]{0,1:T(8,128)S(1)} fusion(bf16[960,1024]{1,0:T(8,128)(2,1)S(1)} %bitcast.48, f32[1024,1024]{1,0:T(8,128)S(1)} %copy-done.27), kind=kOutput, calls=%fused_computation.4 | convolution fusion | flops 2016411648 | bytes 10092544 | tf_op jit(solution)/shard_map/dot_general | solution.py:314
  68.1 0.0 copy-start.7
  68.1 0.7 copy-done.20
  68.9 2.5 %collective-permute-start.13 = (bf16[128,1024]{1,0:T(8,128)(2,1)}, bf16[128,1024]{1,0:T(8,128)(2,1)S(1)}, u32[]{:S(2)}, u32[]{:S(2)}) collective-permute-start(bf16[128,1024]{1,0:T(8,128)(2,1)} %collective-permute-done.11.refs_5_), channel_id=1, source_target_pairs={{0,4},{1,3},{4,8},{5,1},{8,12},{9,5},{12,14},{13,9},{14,10},{15,13... | collective-permute-start | bytes 786440 | tf_op jit(solution)/shard_map/ppermute | solution.py:247
  71.4 0.7 copy-done.22
  72.1 0.0 collective-permute-start.18
  72.1 4.1 %bitcast_add_fusion.base = f32[960,1024]{1,0:T(8,128)} fusion(f32[1024,960]{0,1:T(8,128)S(1)} %fusion.1, bf16[960,1024]{1,0:T(8,128)(2,1)S(1)} %bitcast.47, f32[1024,1024]{1,0:T(8,128)S(1)} %copy-done.27), kind=kOutput, calls=%fused_computation.3 | convolution fusion | flops 2016346112 | bytes 14024704 | tf_op jit(solution)/shard_map/dot_general | solution.py:314
  76.2 0.1 stack.174.tab
  76.3 0.1 stack.168.tab
  76.4 0.1 stack.161.tab
  76.5 4.9 %collective-permute-done.13.refs_7_ = bf16[128,1024]{1,0:T(8,128)(2,1)S(1)} collective-permute-done((bf16[128,1024]{1,0:T(8,128)(2,1)}, bf16[128,1024]{1,0:T(8,128)(2,1)S(1)}, u32[]{:S(2)}, u32[]{:S(2)}) %collective-permute-start.13) | collective-permute-done | bytes 262176 | tf_op jit(solution)/shard_map/ppermute | solution.py:247
  81.4 0.7 copy-done.24
  82.1 0.5 collective-permute-start.21
  82.6 1.8 %collective-permute-start.3 = (bf16[480,1024]{1,0:T(8,128)(2,1)}, bf16[480,1024]{1,0:T(8,128)(2,1)}, u32[]{:S(2)}, u32[]{:S(2)}) collective-permute-start(bf16[480,1024]{1,0:T(8,128)(2,1)} %collective-permute-done.2.refs_0_), channel_id=1, source_target_pairs={{0,4},{1,3},{4,8},{5,1},{8,12},{9,5},{12,14},{13,9},{14,10},{15,13... | collective-permute-start | bytes 2949128 | tf_op jit(solution)/shard_map/ppermute | solution.py:247
  84.4 0.1 pad_add_fusion.3.tab
  84.5 0.1 pad_add_fusion.tab
  84.6 0.1 pad_add_fusion.2.tab
  84.7 0.1 pad_add_fusion.1.tab
  84.8 1.2 copy-done.9
  86.0 0.0 copy-start.26
  86.0 1.8 %stage.6.refs_4_ = bf16[7680,1024]{1,0:T(8,128)(2,1)S(1)} custom-call(s32[2]{0:T(128)S(1)} %pad_add_fusion.3.tab, bf16[480,1024]{1,0:T(8,128)(2,1)S(1)} %copy-done.7, bf16[480,1024]{1,0:T(8,128)(2,1)S(1)} %copy-done.9), custom_call_target="tpu_custom_call" | custom-call | bytes 3932160 | tf_op jit(solution)/shard_map/stage/pallas_call | solution.py:217
  87.8 0.2 collective-permute-start.14
  88.0 4.0 %collective-permute-done.18.refs_2_ = bf16[480,1024]{1,0:T(8,128)(2,1)} collective-permute-done((bf16[480,1024]{1,0:T(8,128)(2,1)}, bf16[480,1024]{1,0:T(8,128)(2,1)}, u32[]{:S(2)}, u32[]{:S(2)}) %collective-permute-start.18) | collective-permute-done | bytes 983072 | tf_op jit(solution)/shard_map/ppermute | solution.py:247
  92.1 11.8 %chain.1 = bf16[960,1024]{1,0:T(8,128)(2,1)S(1)} custom-call(s32[16]{0:T(128)S(1)} %stack.161.tab, f32[960,1024]{1,0:T(8,128)S(1)} %copy-done.26, bf16[128,1024]{1,0:T(8,128)(2,1)S(1)} %copy-done.13, bf16[128,1024]{1,0:T(8,128)(2,1)S(1)} %copy-done.15, bf16[128,1024]{1,0:T(8,128)(2,1)S(1)} %copy-done.19, bf16[128,1024]{1,0:T(8,128)(2,1)S(1)} %copy-done.17, ...), custom_call_target="tpu_custom_call" | custom-call | flops 6039797760 | bytes 7864320 | tf_op jit(solution)/shard_map/chain/pallas_call | solution.py:75
  103.9 0.0 slice-start
  104.0 4.0 %stage.7.refs_4_ = bf16[7680,1024]{1,0:T(8,128)(2,1)S(1)} custom-call(s32[4]{0:T(128)S(1)} %pad_add_fusion.2.tab, bf16[480,1024]{1,0:T(8,128)(2,1)} %collective-permute-done.refs_0_, bf16[480,1024]{1,0:T(8,128)(2,1)} %collective-permute-done.22.refs_1_, bf16[480,1024]{1,0:T(8,128)(2,1)} %collective-permute-done.16.refs_2_, ...), custom_call_target="tpu_custom_call", output_to_operand_aliasing={{}: (5, {})} | custom-call | bytes 7864320 | tf_op jit(solution)/shard_map/stage/pallas_call | solution.py:217
  108.0 0.0 slice-start.1
  108.0 0.6 collective-permute-start.4
  108.6 3.0 %stage.8.refs_2_ = bf16[7680,1024]{1,0:T(8,128)(2,1)S(1)} custom-call(s32[4]{0:T(128)S(1)} %pad_add_fusion.1.tab, bf16[480,1024]{1,0:T(8,128)(2,1)} %collective-permute-done.1.refs_0_, bf16[480,1024]{1,0:T(8,128)(2,1)S(1)} %collective-permute-done.20.refs_1_, bf16[480,1024]{1,0:T(8,128)(2,1)} %collective-permute-done.17.refs_2_, ...), custom_call_target="tpu_custom_call", output_to_operand_aliasing={{}: (5, {})} | custom-call | bytes 7864320 | tf_op jit(solution)/shard_map/stage/pallas_call | solution.py:217
  111.7 14.2 %stage.9 = (bf16[7680,1024]{1,0:T(8,128)(2,1)S(1)}, bf16[2,480,7680]{2,1,0:T(8,128)(2,1)}) custom-call(s32[5]{0:T(128)S(1)} %stack.174.tab, bf16[2,480,1024]{2,1,0:T(8,128)(2,1)S(1)} %bitcast.51, bf16[480,7680]{1,0:T(8,128)(2,1)S(1)} %bitcast.50, bf16[7680,1024]{1,0:T(8,128)(2,1)S(1)} %stage.8.refs_2_), custom_call_target="tpu_custom_call", output_to_operand_aliasing={{0}: (3, {})} | custom-call | flops 10066329600 | bytes 41943040 | tf_op jit(solution)/shard_map/stage/pallas_call | solution.py:217
  125.9 5.4 %copy-done.2 = bf16[7680,1024]{1,0:T(8,128)(2,1)} copy-done((bf16[7680,1024]{1,0:T(8,128)(2,1)}, bf16[7680,1024]{1,0:T(8,128)(2,1)S(1)}, u32[]{:S(2)}) %copy-start.2) | copy-done | bytes 15728664
  131.3 1.0 copy-done.10
  132.2 5.5 %copy-done.3 = bf16[7680,1024]{1,0:T(8,128)(2,1)S(1)} copy-done((bf16[7680,1024]{1,0:T(8,128)(2,1)S(1)}, bf16[7680,1024]{1,0:T(8,128)(2,1)}, u32[]{:S(2)}) %copy-start.3) | copy-done | bytes 15728664
  137.7 3.1 %copy-done.4 = bf16[480,7680]{1,0:T(8,128)(2,1)S(1)} copy-done((bf16[480,7680]{1,0:T(8,128)(2,1)S(1)}, bf16[480,7680]{1,0:T(8,128)(2,1)}, u32[]{:S(2)}) %copy-start.4) | copy-done | bytes 7372824
  140.8 1.5 copy-done.6
  142.4 1.2 copy-done.11
  143.6 9.3 %stage.10 = (bf16[7680,1024]{1,0:T(8,128)(2,1)S(1)}, bf16[2,480,7680]{2,1,0:T(8,128)(2,1)}) custom-call(s32[6]{0:T(128)S(1)} %stack.168.tab, bf16[480,1024]{1,0:T(8,128)(2,1)} %collective-permute-done.2.refs_0_, bf16[480,1024]{1,0:T(8,128)(2,1)S(1)} %collective-permute-done.14.refs_1_, ...), custom_call_target="tpu_custom_call", output_to_operand_aliasing={{0}: (7, {}), {1}: (8, {})} | custom-call | flops 4026531840 | bytes 24641536 | tf_op jit(solution)/shard_map/stage/pallas_call | solution.py:217
  152.9 0.0 copy-start.1
  152.9 6.2 %stage.11 = (bf16[7680,1024]{1,0:T(8,128)(2,1)S(1)}, bf16[2,480,7680]{2,1,0:T(8,128)(2,1)}) custom-call(s32[3]{0:T(128)S(1)} %pad_add_fusion.tab, bf16[480,1024]{1,0:T(8,128)(2,1)} %collective-permute-done.3.refs_0_, bf16[480,1024]{1,0:T(8,128)(2,1)} %collective-permute-done.4.refs_1_, ...), custom_call_target="tpu_custom_call", output_to_operand_aliasing={{0}: (5, {}), {1}: (6, {})} | custom-call | flops 2013265920 | bytes 12320768 | tf_op jit(solution)/shard_map/stage/pallas_call | solution.py:217
  (65 shorter events, 0.2 us)
Async XLA Ops:
  0.0 65.9 %copy-start = (bf16[2,480,1024]{2,1,0:T(8,128)(2,1)S(1)}, bf16[2,480,1024]{2,1,0:T(8,128)(2,1)}, u32[]{:S(2)}) copy-start(bf16[2,480,1024]{2,1,0:T(8,128)(2,1)} %param.6) | copy-start | bytes 5898244
  0.0 6.7 %collective-permute-start.15 = (bf16[480,1024]{1,0:T(8,128)(2,1)}, bf16[480,1024]{1,0:T(8,128)(2,1)S(1)}, u32[]{:S(2)}, u32[]{:S(2)}) collective-permute-start(bf16[480,1024]{1,0:T(8,128)(2,1)} %refs_0_.1), channel_id=1, source_target_pairs={{0,1},{1,0},{2,3},{3,2},{4,5},{5,4},{6,7},{7,6},{8,9},{9,8},{10,11... | collective-permute-start | bytes 2949128 | tf_op jit(solution)/shard_map/ppermute | solution.py:248
  0.5 26.4 %collective-permute-start = (bf16[480,1024]{1,0:T(8,128)(2,1)}, bf16[480,1024]{1,0:T(8,128)(2,1)}, u32[]{:S(2)}, u32[]{:S(2)}) collective-permute-start(bf16[480,1024]{1,0:T(8,128)(2,1)} %refs_0_.1), channel_id=1, source_target_pairs={{0,4},{1,3},{4,8},{5,1},{8,12},{9,5},{12,14},{13,9},{14,10},{15,13... | collective-permute-start | bytes 2949128 | tf_op jit(solution)/shard_map/ppermute | solution.py:247
  4.1 13.7 %collective-permute-start.5 = (bf16[64,1024]{1,0:T(8,128)(2,1)S(1)}, bf16[64,1024]{1,0:T(8,128)(2,1)S(1)}, u32[]{:S(2)}, u32[]{:S(2)}) collective-permute-start(bf16[64,1024]{1,0:T(8,128)(2,1)S(1)} %dynamic-slice_convert_fusion), channel_id=1, source_target_pairs={{0,8},{1,9},{2,10},{3,11},{4,12},{5,13},{6,14},{7,15},{8,0},{9,1},... | collective-permute-start | bytes 393224 | tf_op jit(solution)/shard_map/ppermute | solution.py:249
  6.7 59.2 %copy-start.27 = (f32[1024,1024]{1,0:T(8,128)S(1)}, f32[1024,1024]{1,0:T(8,128)}, u32[]{:S(2)}) copy-start(f32[1024,1024]{1,0:T(8,128)} %param.9) | copy-start | bytes 12582916
  6.7 59.1 %copy-start.8 = (bf16[480,1024]{1,0:T(8,128)(2,1)}, bf16[480,1024]{1,0:T(8,128)(2,1)S(1)}, u32[]{:S(2)}) copy-start(bf16[480,1024]{1,0:T(8,128)(2,1)S(1)} %collective-permute-done.15.refs_1_) | copy-start | bytes 2949124
  6.8 39.3 %collective-permute-start.16 = (bf16[480,1024]{1,0:T(8,128)(2,1)S(1)}, bf16[480,1024]{1,0:T(8,128)(2,1)}, u32[]{:S(2)}, u32[]{:S(2)}) collective-permute-start(bf16[480,1024]{1,0:T(8,128)(2,1)S(1)} %collective-permute-done.15.refs_1_), channel_id=1, source_target_pairs={{0,4},{1,3},{4,8},{5,1},{8,12},{9,5},{12,14},{13,9},{14,10},{15,13... | collective-permute-start | bytes 2949128 | tf_op jit(solution)/shard_map/ppermute | solution.py:247
  22.7 5.1 %collective-permute-start.6 = (bf16[64,1024]{1,0:T(8,128)(2,1)S(1)}, bf16[64,1024]{1,0:T(8,128)(2,1)S(1)}, u32[]{:S(2)}, u32[]{:S(2)}) collective-permute-start(bf16[64,1024]{1,0:T(8,128)(2,1)S(1)} %fusion.4), channel_id=1, source_target_pairs={{0,1},{1,0},{2,3},{3,2},{4,5},{5,4},{6,7},{7,6},{8,9},{9,8},{10,11... | collective-permute-start | bytes 393224 | tf_op jit(solution)/shard_map/ppermute | solution.py:248
  26.9 37.2 %collective-permute-start.1 = (bf16[480,1024]{1,0:T(8,128)(2,1)}, bf16[480,1024]{1,0:T(8,128)(2,1)}, u32[]{:S(2)}, u32[]{:S(2)}) collective-permute-start(bf16[480,1024]{1,0:T(8,128)(2,1)} %collective-permute-done.refs_0_), channel_id=1, source_target_pairs={{0,4},{1,3},{4,8},{5,1},{8,12},{9,5},{12,14},{13,9},{14,10},{15,13... | collective-permute-start | bytes 2949128 | tf_op jit(solution)/shard_map/ppermute | solution.py:247
  27.9 16.4 %collective-permute-start.7 = (bf16[128,1024]{1,0:T(8,128)(2,1)S(1)}, bf16[128,1024]{1,0:T(8,128)(2,1)S(1)}, u32[]{:S(2)}, u32[]{:S(2)}) collective-permute-start(bf16[128,1024]{1,0:T(8,128)(2,1)S(1)} %pad_maximum_fusion.refs_0_), channel_id=1, source_target_pairs={{0,4},{1,3},{4,8},{5,1},{8,12},{9,5},{12,14},{13,9},{14,10},{15,13... | collective-permute-start | bytes 786440 | tf_op jit(solution)/shard_map/ppermute | solution.py:247
  28.6 0.7 copy-start.12
  44.3 6.4 %collective-permute-start.9 = (bf16[128,1024]{1,0:T(8,128)(2,1)S(1)}, bf16[128,1024]{1,0:T(8,128)(2,1)S(1)}, u32[]{:S(2)}, u32[]{:S(2)}) collective-permute-start(bf16[128,1024]{1,0:T(8,128)(2,1)S(1)} %collective-permute-done.7.refs_1_), channel_id=1, source_target_pairs={{0,4},{1,3},{4,8},{5,1},{8,12},{9,5},{12,14},{13,9},{14,10},{15,13... | collective-permute-start | bytes 786440 | tf_op jit(solution)/shard_map/ppermute | solution.py:247
  46.1 26.0 %collective-permute-start.17 = (bf16[480,1024]{1,0:T(8,128)(2,1)}, bf16[480,1024]{1,0:T(8,128)(2,1)}, u32[]{:S(2)}, u32[]{:S(2)}) collective-permute-start(bf16[480,1024]{1,0:T(8,128)(2,1)} %collective-permute-done.16.refs_2_), channel_id=1, source_target_pairs={{0,4},{1,3},{4,8},{5,1},{8,12},{9,5},{12,14},{13,9},{14,10},{15,13... | collective-permute-start | bytes 2949128 | tf_op jit(solution)/shard_map/ppermute | solution.py:247
  48.5 3.9 %collective-permute-start.8 = (bf16[128,1024]{1,0:T(8,128)(2,1)S(1)}, bf16[128,1024]{1,0:T(8,128)(2,1)S(1)}, u32[]{:S(2)}, u32[]{:S(2)}) collective-permute-start(bf16[128,1024]{1,0:T(8,128)(2,1)S(1)} %collective-permute-done.7.refs_1_), channel_id=1, source_target_pairs={{0,1},{1,0},{2,3},{3,2},{4,5},{5,4},{6,7},{7,6},{8,9},{9,8},{10,11... | collective-permute-start | bytes 786440 | tf_op jit(solution)/shard_map/ppermute | solution.py:248
  48.5 0.7 copy-start.14
  50.6 17.5 %copy-start.16 = (bf16[128,1024]{1,0:T(8,128)(2,1)}, bf16[128,1024]{1,0:T(8,128)(2,1)S(1)}, u32[]{:S(2)}) copy-start(bf16[128,1024]{1,0:T(8,128)(2,1)S(1)} %collective-permute-done.9.refs_3_) | copy-start | bytes 786436
  50.6 13.4 %collective-permute-start.11 = (bf16[128,1024]{1,0:T(8,128)(2,1)S(1)}, bf16[128,1024]{1,0:T(8,128)(2,1)}, u32[]{:S(2)}, u32[]{:S(2)}) collective-permute-start(bf16[128,1024]{1,0:T(8,128)(2,1)S(1)} %collective-permute-done.9.refs_3_), channel_id=1, source_target_pairs={{0,4},{1,3},{4,8},{5,1},{8,12},{9,5},{12,14},{13,9},{14,10},{15,13... | collective-permute-start | bytes 786440 | tf_op jit(solution)/shard_map/ppermute | solution.py:247
  52.4 15.7 %collective-permute-start.10 = (bf16[128,1024]{1,0:T(8,128)(2,1)S(1)}, bf16[128,1024]{1,0:T(8,128)(2,1)S(1)}, u32[]{:S(2)}, u32[]{:S(2)}) collective-permute-start(bf16[128,1024]{1,0:T(8,128)(2,1)S(1)} %collective-permute-done.9.refs_3_), channel_id=1, source_target_pairs={{0,1},{1,0},{2,3},{3,2},{4,5},{5,4},{6,7},{7,6},{8,9},{9,8},{10,11... | collective-permute-start | bytes 786440 | tf_op jit(solution)/shard_map/ppermute | solution.py:248
  52.4 0.7 copy-start.18
  53.2 28.9 %collective-permute-start.22 = (bf16[480,1024]{1,0:T(8,128)(2,1)}, bf16[480,1024]{1,0:T(8,128)(2,1)}, u32[]{:S(2)}, u32[]{:S(2)}) collective-permute-start(bf16[480,1024]{1,0:T(8,128)(2,1)} %collective-permute-done.refs_0_), channel_id=1, source_target_pairs={{0,1},{1,0},{2,3},{3,2},{4,5},{5,4},{6,7},{7,6},{8,9},{9,8},{10,11... | collective-permute-start | bytes 2949128 | tf_op jit(solution)/shard_map/ppermute | solution.py:248
  64.1 7.3 %collective-permute-start.12 = (bf16[128,1024]{1,0:T(8,128)(2,1)}, bf16[128,1024]{1,0:T(8,128)(2,1)S(1)}, u32[]{:S(2)}, u32[]{:S(2)}) collective-permute-start(bf16[128,1024]{1,0:T(8,128)(2,1)} %collective-permute-done.11.refs_5_), channel_id=1, source_target_pairs={{0,1},{1,0},{2,3},{3,2},{4,5},{5,4},{6,7},{7,6},{8,9},{9,8},{10,11... | collective-permute-start | bytes 786440 | tf_op jit(solution)/shard_map/ppermute | solution.py:248
  64.1 18.5 %collective-permute-start.2 = (bf16[480,1024]{1,0:T(8,128)(2,1)}, bf16[480,1024]{1,0:T(8,128)(2,1)}, u32[]{:S(2)}, u32[]{:S(2)}) collective-permute-start(bf16[480,1024]{1,0:T(8,128)(2,1)} %collective-permute-done.1.refs_0_), channel_id=1, source_target_pairs={{0,4},{1,3},{4,8},{5,1},{8,12},{9,5},{12,14},{13,9},{14,10},{15,13... | collective-permute-start | bytes 2949128 | tf_op jit(solution)/shard_map/ppermute | solution.py:247
  68.1 16.6 %copy-start.7 = (bf16[480,1024]{1,0:T(8,128)(2,1)S(1)}, bf16[480,1024]{1,0:T(8,128)(2,1)}, u32[]{:S(2)}) copy-start(bf16[480,1024]{1,0:T(8,128)(2,1)} %refs_0_.1) | copy-start | bytes 2949124
  68.1 0.7 copy-start.20
  68.9 12.5 %collective-permute-start.13 = (bf16[128,1024]{1,0:T(8,128)(2,1)}, bf16[128,1024]{1,0:T(8,128)(2,1)S(1)}, u32[]{:S(2)}, u32[]{:S(2)}) collective-permute-start(bf16[128,1024]{1,0:T(8,128)(2,1)} %collective-permute-done.11.refs_5_), channel_id=1, source_target_pairs={{0,4},{1,3},{4,8},{5,1},{8,12},{9,5},{12,14},{13,9},{14,10},{15,13... | collective-permute-start | bytes 786440 | tf_op jit(solution)/shard_map/ppermute | solution.py:247
  71.4 0.7 copy-start.22
  72.1 15.8 %collective-permute-start.23 = (bf16[480,1024]{1,0:T(8,128)(2,1)}, bf16[480,1024]{1,0:T(8,128)(2,1)}, u32[]{:S(2)}, u32[]{:S(2)}) collective-permute-start(bf16[480,1024]{1,0:T(8,128)(2,1)} %collective-permute-done.16.refs_2_), channel_id=1, source_target_pairs={{0,1},{1,0},{2,3},{3,2},{4,5},{5,4},{6,7},{7,6},{8,9},{9,8},{10,11... | collective-permute-start | bytes 2949128 | tf_op jit(solution)/shard_map/ppermute | solution.py:248
  72.1 19.9 %collective-permute-start.18 = (bf16[480,1024]{1,0:T(8,128)(2,1)}, bf16[480,1024]{1,0:T(8,128)(2,1)}, u32[]{:S(2)}, u32[]{:S(2)}) collective-permute-start(bf16[480,1024]{1,0:T(8,128)(2,1)} %collective-permute-done.17.refs_2_), channel_id=1, source_target_pairs={{0,4},{1,3},{4,8},{5,1},{8,12},{9,5},{12,14},{13,9},{14,10},{15,13... | collective-permute-start | bytes 2949128 | tf_op jit(solution)/shard_map/ppermute | solution.py:247
  81.4 0.7 copy-start.24
  82.1 26.5 %collective-permute-start.20 = (bf16[480,1024]{1,0:T(8,128)(2,1)}, bf16[480,1024]{1,0:T(8,128)(2,1)S(1)}, u32[]{:S(2)}, u32[]{:S(2)}) collective-permute-start(bf16[480,1024]{1,0:T(8,128)(2,1)} %collective-permute-done.1.refs_0_), channel_id=1, source_target_pairs={{0,1},{1,0},{2,3},{3,2},{4,5},{5,4},{6,7},{7,6},{8,9},{9,8},{10,11... | collective-permute-start | bytes 2949128 | tf_op jit(solution)/shard_map/ppermute | solution.py:248
  82.1 26.5 %collective-permute-start.21 = (bf16[480,1024]{1,0:T(8,128)(2,1)}, bf16[480,1024]{1,0:T(8,128)(2,1)S(1)}, u32[]{:S(2)}, u32[]{:S(2)}) collective-permute-start(bf16[480,1024]{1,0:T(8,128)(2,1)} %collective-permute-done.17.refs_2_), channel_id=1, source_target_pairs={{0,1},{1,0},{2,3},{3,2},{4,5},{5,4},{6,7},{7,6},{8,9},{9,8},{10,11... | collective-permute-start | bytes 2949128 | tf_op jit(solution)/shard_map/ppermute | solution.py:248
  82.6 25.4 %collective-permute-start.3 = (bf16[480,1024]{1,0:T(8,128)(2,1)}, bf16[480,1024]{1,0:T(8,128)(2,1)}, u32[]{:S(2)}, u32[]{:S(2)}) collective-permute-start(bf16[480,1024]{1,0:T(8,128)(2,1)} %collective-permute-done.2.refs_0_), channel_id=1, source_target_pairs={{0,4},{1,3},{4,8},{5,1},{8,12},{9,5},{12,14},{13,9},{14,10},{15,13... | collective-permute-start | bytes 2949128 | tf_op jit(solution)/shard_map/ppermute | solution.py:247
  84.8 1.2 copy-start.9
  86.0 6.1 %copy-start.13 = (bf16[128,1024]{1,0:T(8,128)(2,1)S(1)}, bf16[128,1024]{1,0:T(8,128)(2,1)}, u32[]{:S(2)}) copy-start(bf16[128,1024]{1,0:T(8,128)(2,1)} %copy-done.12) | copy-start | bytes 786436
  86.0 6.1 %copy-start.15 = (bf16[128,1024]{1,0:T(8,128)(2,1)S(1)}, bf16[128,1024]{1,0:T(8,128)(2,1)}, u32[]{:S(2)}) copy-start(bf16[128,1024]{1,0:T(8,128)(2,1)} %copy-done.14) | copy-start | bytes 786436
  86.0 6.1 %copy-start.17 = (bf16[128,1024]{1,0:T(8,128)(2,1)S(1)}, bf16[128,1024]{1,0:T(8,128)(2,1)}, u32[]{:S(2)}) copy-start(bf16[128,1024]{1,0:T(8,128)(2,1)} %copy-done.16) | copy-start | bytes 786436
  86.0 6.1 %copy-start.19 = (bf16[128,1024]{1,0:T(8,128)(2,1)S(1)}, bf16[128,1024]{1,0:T(8,128)(2,1)}, u32[]{:S(2)}) copy-start(bf16[128,1024]{1,0:T(8,128)(2,1)} %copy-done.18) | copy-start | bytes 786436
  86.0 6.1 %copy-start.21 = (bf16[128,1024]{1,0:T(8,128)(2,1)S(1)}, bf16[128,1024]{1,0:T(8,128)(2,1)}, u32[]{:S(2)}) copy-start(bf16[128,1024]{1,0:T(8,128)(2,1)} %copy-done.20) | copy-start | bytes 786436
  86.0 6.1 %copy-start.23 = (bf16[128,1024]{1,0:T(8,128)(2,1)S(1)}, bf16[128,1024]{1,0:T(8,128)(2,1)}, u32[]{:S(2)}) copy-start(bf16[128,1024]{1,0:T(8,128)(2,1)} %copy-done.22) | copy-start | bytes 786436
  86.0 6.1 %copy-start.25 = (bf16[128,1024]{1,0:T(8,128)(2,1)S(1)}, bf16[128,1024]{1,0:T(8,128)(2,1)}, u32[]{:S(2)}) copy-start(bf16[128,1024]{1,0:T(8,128)(2,1)} %copy-done.24) | copy-start | bytes 786436
  86.0 6.1 %copy-start.26 = (f32[960,1024]{1,0:T(8,128)S(1)}, f32[960,1024]{1,0:T(8,128)}, u32[]{:S(2)}) copy-start(f32[960,1024]{1,0:T(8,128)} %bitcast_add_fusion.base) | copy-start | bytes 11796484
  87.8 43.4 %collective-permute-start.14 = (bf16[480,1024]{1,0:T(8,128)(2,1)}, bf16[480,1024]{1,0:T(8,128)(2,1)S(1)}, u32[]{:S(2)}, u32[]{:S(2)}) collective-permute-start(bf16[480,1024]{1,0:T(8,128)(2,1)} %collective-permute-done.2.refs_0_), channel_id=1, source_target_pairs={{0,1},{1,0},{2,3},{3,2},{4,5},{5,4},{6,7},{7,6},{8,9},{9,8},{10,11... | collective-permute-start | bytes 2949128 | tf_op jit(solution)/shard_map/ppermute | solution.py:248
  92.0 39.3 %collective-permute-start.19 = (bf16[480,1024]{1,0:T(8,128)(2,1)}, bf16[480,1024]{1,0:T(8,128)(2,1)S(1)}, u32[]{:S(2)}, u32[]{:S(2)}) collective-permute-start(bf16[480,1024]{1,0:T(8,128)(2,1)} %collective-permute-done.18.refs_2_), channel_id=1, source_target_pairs={{0,1},{1,0},{2,3},{3,2},{4,5},{5,4},{6,7},{7,6},{8,9},{9,8},{10,11... | collective-permute-start | bytes 2949128 | tf_op jit(solution)/shard_map/ppermute | solution.py:248
  103.9 7.7 %copy-start.5 = (bf16[960,1024]{1,0:T(8,128)(2,1)}, bf16[960,1024]{1,0:T(8,128)(2,1)S(1)}, u32[]{:S(2)}) copy-start(bf16[960,1024]{1,0:T(8,128)(2,1)S(1)} %chain.1) | copy-start | bytes 5898244
  103.9 7.7 %slice-start = ((s8[7372800]{0:T(1024)(128)(4,1)}), s8[4194304]{0:T(1024)(128)(4,1)S(1)}, s32[]{:S(2)}) async-start(s8[7372800]{0:T(1024)(128)(4,1)} %bitcast.49), calls=%async_computation | async-start | bytes 8388608
  108.0 3.7 %slice-start.1 = ((s8[7372800]{0:T(1024)(128)(4,1)}), s8[3178496]{0:T(1024)(128)(4,1)S(1)}, s32[]{:S(2)}) async-start(s8[7372800]{0:T(1024)(128)(4,1)} %bitcast.49), calls=%async_computation.1 | async-start | bytes 6356992
  108.0 44.8 %collective-permute-start.4 = (bf16[480,1024]{1,0:T(8,128)(2,1)}, bf16[480,1024]{1,0:T(8,128)(2,1)}, u32[]{:S(2)}, u32[]{:S(2)}) collective-permute-start(bf16[480,1024]{1,0:T(8,128)(2,1)} %collective-permute-done.3.refs_0_), channel_id=1, source_target_pairs={{0,1},{1,0},{2,3},{3,2},{4,5},{5,4},{6,7},{7,6},{8,9},{9,8},{10,11... | collective-permute-start | bytes 2949128 | tf_op jit(solution)/shard_map/ppermute | solution.py:248
  125.9 5.4 %copy-start.2 = (bf16[7680,1024]{1,0:T(8,128)(2,1)}, bf16[7680,1024]{1,0:T(8,128)(2,1)S(1)}, u32[]{:S(2)}) copy-start(bf16[7680,1024]{1,0:T(8,128)(2,1)S(1)} %get-tuple-element.10.refs_6_) | copy-start | bytes 47185924
  131.3 1.0 copy-start.10
  132.2 5.5 %copy-start.3 = (bf16[7680,1024]{1,0:T(8,128)(2,1)S(1)}, bf16[7680,1024]{1,0:T(8,128)(2,1)}, u32[]{:S(2)}) copy-start(bf16[7680,1024]{1,0:T(8,128)(2,1)} %copy-done.2) | copy-start | bytes 47185924
  137.7 3.1 %copy-start.4 = (bf16[480,7680]{1,0:T(8,128)(2,1)S(1)}, bf16[480,7680]{1,0:T(8,128)(2,1)}, u32[]{:S(2)}) copy-start(bf16[480,7680]{1,0:T(8,128)(2,1)} %refs_3_.1) | copy-start | bytes 22118404
  140.8 1.5 copy-start.6
  142.4 1.2 copy-start.11
  152.9 6.2 %copy-start.1 = (bf16[2,480,1024]{2,1,0:T(8,128)(2,1)S(1)}, bf16[2,480,1024]{2,1,0:T(8,128)(2,1)}, u32[]{:S(2)}) copy-start(bf16[2,480,1024]{2,1,0:T(8,128)(2,1)} %param.6) | copy-start | bytes 5898244
